TPU v7x, 256 devices: a whole 4x4x8 slice. The times are simulated.
256 devices in a mesh: rep: 32 (over y, z), tp: 8 (over x, core).
Axes of the slice: x: 4, y: 4, z: 8, core: 2. Of those that a mesh axis runs over, the one named last changes fastest.
Arguments:
- reference_rows: bfloat16 [32768, 8192], P('rep', 'tp'), may hold values from -7 to 7
- critic_rows: bfloat16 [32768, 4096], P('rep', 'tp'), may hold values from -7 to 7
- segment_ids: int32 [32768], P('rep'), may hold values from -1 to 32767, as said below
- pack_dest: int32 [32, 32], P('rep'), may hold values from 0 to 31, as said below
- ref_query: bfloat16 [8192, 4096], P('rep', 'tp'), may hold values from -2 to 2
- ref_key: bfloat16 [8192, 1024], P('rep', 'tp'), may hold values from -2 to 2
- ref_value: bfloat16 [8192, 1024], P('rep', 'tp'), may hold values from -0.0625 to 0.0625
- critic_query: bfloat16 [4096, 4096], P(None, 'tp'), may hold values from -2 to 2
- critic_key: bfloat16 [4096, 1024], P(None, 'tp'), may hold values from -2 to 2
- critic_value: bfloat16 [4096, 1024], P(None, 'tp'), may hold values from -0.09375 to 0.09375
- ref_readout: bfloat16 [4096], P('tp'), may hold values from -0.09375 to 0.09375
- critic_readout: bfloat16 [4096], P('tp'), may hold values from -0.09375 to 0.09375
Outputs:
- ref_score: float32 [32768], P('rep')
- value: float32 [32768], P('rep')
Inputs may be any that keep to these rules, and one draw needn't show every extreme that they name: Each row is a permutation: block b of replica s goes to pack pack_dest[s, b]. `segment_ids`: in every aligned block of 32 slots the used rows come first and the rest hold -1; a block holds 1 to 31 used rows, and every pack receives exactly 31 used rows from some replica and exactly 512 used rows in all. A rollout is a run of consecutive used rows with one id inside one block; different rollouts have different ids.
All inputs are finite; a program needn't handle non-finite values.
Results may differ from a plain program's by a relative error of at most 0.0084.
Values may be sent and summed in bfloat16 or wider, within the bound.
No kernel may reach another device: no remote copies, remote signals or barrier semaphores. Data moves between devices by JAX's collectives and lax.ppermute only.
A program may use at most 128 MiB of HBM per device.

v0:
```python
import jax
import jax.numpy as jnp
from jax import lax
from jax.sharding import PartitionSpec as P

HD = 128


def normalize(source):
    widened = source.astype(jnp.float32)
    scale_row = lax.rsqrt(jnp.mean(widened * widened, axis=-1, keepdims=True) + 1e-05)
    return (widened * scale_row).astype(jnp.bfloat16)


def attend(queries, keys_in, values_in, segments):
    row_count = queries.shape[0]
    groups = keys_in.shape[1] // HD
    shared = queries.shape[1] // keys_in.shape[1]
    query_four = queries.reshape(row_count, groups, shared, HD)
    key_three = keys_in.reshape(row_count, groups, HD)
    value_three = values_in.reshape(row_count, groups, HD)
    scores = jnp.einsum(
        "pgjd,qgd->gjpq", query_four, key_three, preferred_element_type=jnp.float32
    ) * HD ** (-0.5)
    position = jnp.arange(row_count)
    allowed = (position[None, :] <= position[:, None]) & (segments[:, None] == segments[None, :])
    masked = jnp.where(allowed, scores, -1e30)
    row_max = jnp.max(masked, axis=-1, keepdims=True)
    powers = jnp.where(allowed, jnp.exp(masked - row_max), 0.0)
    weights = (powers / jnp.sum(powers, axis=-1, keepdims=True)).astype(jnp.bfloat16)
    mixture = jnp.einsum("gjpq,qgd->pgjd", weights, value_three, preferred_element_type=jnp.float32)
    return mixture.reshape(row_count, groups * shared * HD).astype(jnp.bfloat16)


def compact_index(segments):
    row_count = segments.shape[0]
    sort_keys = jnp.where(segments >= 0, 0, row_count).astype(jnp.int32) + jnp.arange(
        row_count, dtype=jnp.int32
    )
    return jnp.argsort(sort_keys)[: row_count // 2]


def project(normed, weight):
    return jnp.dot(normed, weight, preferred_element_type=jnp.float32).astype(jnp.bfloat16)


def body(
    reference_rows,
    critic_rows,
    segment_ids,
    pack_dest,
    ref_query,
    ref_key,
    ref_value,
    critic_query,
    critic_key,
    critic_value,
    ref_readout,
    critic_readout,
):
    replicas = lax.axis_size("rep")
    slot_count = segment_ids.shape[0]
    block_rows = slot_count // replicas
    destination = pack_dest[0]
    inverse = jnp.argsort(destination)

    def by_pack(source):
        blocks = source.reshape((replicas, block_rows) + source.shape[1:])
        return jnp.take(blocks, inverse, axis=0).reshape(source.shape)

    ref_in, critic_in, ids_in = (
        lax.all_to_all(by_pack(reference_rows), "rep", split_axis=0, concat_axis=0, tiled=True),
        lax.all_to_all(by_pack(critic_rows), "rep", split_axis=0, concat_axis=0, tiled=True),
        lax.all_to_all(by_pack(segment_ids), "rep", split_axis=0, concat_axis=0, tiled=True),
    )
    chosen = compact_index(ids_in)
    pack_ids = ids_in[chosen]
    ref_full, critic_full = (
        lax.all_gather(ref_in[chosen], "tp", axis=1, tiled=True),
        lax.all_gather(critic_in[chosen], "tp", axis=1, tiled=True),
    )
    critic_normed = normalize(critic_full)
    critic_attn = attend(
        project(critic_normed, critic_query),
        project(critic_normed, critic_key),
        project(critic_normed, critic_value),
        pack_ids,
    )
    ref_normed = normalize(ref_full)
    pieces = (
        lax.all_gather(ref_query, "rep", axis=0, tiled=True),
        lax.all_gather(ref_key, "rep", axis=0, tiled=True),
        lax.all_gather(ref_value, "rep", axis=0, tiled=True),
    )
    ref_q, ref_k, ref_v = tuple(
        (
            jnp.dot(ref_normed, weight_piece, preferred_element_type=jnp.float32)
            for weight_piece in pieces
        )
    )
    ref_attn = attend(
        ref_q.astype(jnp.bfloat16), ref_k.astype(jnp.bfloat16), ref_v.astype(jnp.bfloat16), pack_ids
    )
    ref_spread = jnp.zeros((slot_count, ref_attn.shape[1]), jnp.bfloat16).at[chosen].set(ref_attn)
    critic_spread = (
        jnp.zeros((slot_count, critic_attn.shape[1]), jnp.bfloat16).at[chosen].set(critic_attn)
    )
    ref_home, critic_home = (
        lax.all_to_all(ref_spread, "rep", split_axis=0, concat_axis=0, tiled=True),
        lax.all_to_all(critic_spread, "rep", split_axis=0, concat_axis=0, tiled=True),
    )
    ref_home = jnp.take(ref_home.reshape(replicas, block_rows, -1), destination, axis=0).reshape(
        slot_count, -1
    )
    critic_home = jnp.take(
        critic_home.reshape(replicas, block_rows, -1), destination, axis=0
    ).reshape(slot_count, -1)
    partial_value = jnp.stack(
        [
            jnp.dot(ref_home, ref_readout, preferred_element_type=jnp.float32),
            jnp.dot(critic_home, critic_readout, preferred_element_type=jnp.float32),
        ]
    )
    ordered = lax.psum(partial_value, "tp")
    ordered = jnp.where(segment_ids[None, :] >= 0, ordered, 0.0)
    return (ordered[0], ordered[1])


def solution(mesh):
    return jax.shard_map(
        body,
        mesh=mesh,
        in_specs=(
            P("rep", "tp"),
            P("rep", "tp"),
            P("rep"),
            P("rep", None),
            P("rep", "tp"),
            P("rep", "tp"),
            P("rep", "tp"),
            P(None, "tp"),
            P(None, "tp"),
            P(None, "tp"),
            P("tp"),
            P("tp"),
        ),
        out_specs=(P("rep"), P("rep")),
        check_vma=False,
    )
```

profile of v0, /device:TPU:1, one launch (start us, length us, event | category | flops | bytes accessed | tf_op | source)
XLA Modules:
  0.0 513.6 jit_solution(6631517655676095522)
XLA Ops:
  7.2 2.4 sort.34
  9.6 0.8 reshape.165
  10.4 0.6 gather_fusion
  10.9 0.7 bitcast_select_fusion.2
  11.6 12.0 %all-to-all-start = ((s32[32,32,1]{1,2,0:T(1,128)}), s32[32,32,1]{1,2,0:T(1,128)S(1)}, u32[]{:S(2)}, u32[]{:S(2)}) async-start(s32[32,32,1]{1,2,0:T(1,128)} %bitcast.2), calls=%async_computation | async-start | bytes 32768 | tf_op jit(solution)/shard_map/all_to_all | solution.py:74
  23.7 1.8 gather_fusion.6
  25.5 1.2 broadcast_select_fusion.1
  26.7 5.6 %all-to-all-done = s32[32,32,1]{1,2,0:T(1,128)S(1)} async-done(((s32[32,32,1]{1,2,0:T(1,128)}), s32[32,32,1]{1,2,0:T(1,128)S(1)}, u32[]{:S(2)}, u32[]{:S(2)}) %all-to-all-start) | async-done | bytes 4128 | tf_op jit(solution)/shard_map/all_to_all | solution.py:74
  32.3 3.9 all-to-all-start.3
  36.3 0.5 broadcast.155
  36.8 0.7 reduce.7
  37.6 4.4 sort.35
  41.9 18.7 %all-to-all-done.3 = bf16[32,32,512]{2,1,0:T(8,128)(2,1)S(1)} async-done(((bf16[32,32,512]{2,1,0:T(8,128)(2,1)}), bf16[32,32,512]{2,1,0:T(8,128)(2,1)S(1)}, u32[]{:S(2)}, u32[]{:S(2)}) %all-to-all-start.3) | async-done | bytes 1048608 | tf_op jit(solution)/shard_map/all_to_all | solution.py:73
  60.6 2.6 gather_fusion.4
  63.3 2.0 gather_fusion.1
  65.4 1.8 broadcast_select_fusion
  67.2 55.1 %all_to_all.45 = bf16[32,32,1024]{2,1,0:T(8,128)(2,1)} all-to-all(bf16[32,32,1024]{2,1,0:T(8,128)(2,1)S(1)} %broadcast_select_fusion), channel_id=1, replica_groups=mesh['rep'=32,'tp'=8] {'rep'}, dimensions={0} | all-to-all | bytes 4194304 | tf_op jit(solution)/shard_map/all_to_all | solution.py:72
  122.3 5.4 %gather_fusion.2 = bf16[512,1024]{1,0:T(8,128)(2,1)} fusion(bf16[1024,1024]{1,0:T(8,128)(2,1)} %bitcast.109, s32[1024]{0:T(1024)S(1)} %pad_clamp_fusion.1), kind=kCustom, calls=%fused_computation.5 | custom fusion | bytes 2099200 | tf_op jit(solution)/shard_map/gather | solution.py:79
  127.7 0.7 all-gather.12.cloned.1.call-update
  128.5 0.5 all-gather.10.cloned.1.call-update
  129.0 0.5 all-gather.8.cloned.1.call-update
  129.6 2.8 gather_fusion.3
  132.6 3.2 fusion.2
  136.0 4.7 convolution_convert_fusion
  140.8 40.8 %all-gather.14.cloned.1.call-done = bf16[512,8192]{1,0:T(8,128)(2,1)} async-done(((bf16[512,1024]{1,0:T(8,128)(2,1)}), bf16[512,8192]{1,0:T(8,128)(2,1)}) %all-gather.14.cloned.1.call-update) | async-done | bytes 8388624 | tf_op jit(solution)/shard_map/all_gather | solution.py:79
  181.5 5.1 fusion
  186.6 95.4 %all-gather.12.cloned.1.call-done = bf16[8192,512]{1,0:T(8,128)(2,1)} async-done(((bf16[256,512]{1,0:T(8,128)(2,1)}), bf16[8192,512]{1,0:T(8,128)(2,1)}) %all-gather.12.cloned.1.call-update) | async-done | bytes 8388624 | tf_op jit(solution)/shard_map/all_gather | solution.py:91
  282.1 11.2 %convolution_convert_fusion.1 = bf16[512,512]{0,1:T(8,128)(2,1)} fusion(bf16[8192,512]{1,0:T(8,128)(2,1)} %all-gather.12.cloned.1.call-done, bf16[512,8192]{1,0:T(8,128)(2,1)} %all-gather.14.cloned.1.call-done, f32[512]{0:T(512)S(1)} %add_rsqrt_fusion.1), kind=kOutput, calls=%fused_computation.38 | convolution fusion | flops 4307812352 | bytes 17303552 | tf_op jit(solution)/shard_map/dot_general | solution.py:97
  293.3 62.8 %all-gather.10.cloned.1.call-done = bf16[8192,128]{1,0:T(8,128)(2,1)} async-done(((bf16[256,128]{1,0:T(8,128)(2,1)}), bf16[8192,128]{1,0:T(8,128)(2,1)}) %all-gather.10.cloned.1.call-update) | async-done | bytes 2097168 | tf_op jit(solution)/shard_map/all_gather | solution.py:92
  356.1 10.2 %fusion.4 = (f32[4,512]{1,0:T(4,128)S(1)}, f32[512,512,4]{1,0,2:T(8,128)}) fusion(pred[512,512]{0,1:T(8,128)(4,1)S(1)} %fusion.26, bf16[512,4,128]{0,2,1:T(8,128)(2,1)} %bitcast.122, bf16[8192,128]{1,0:T(8,128)(2,1)} %all-gather.10.cloned.1.call-done, bf16[512,8192]{1,0:T(8,128)(2,1)} %all-gather.14.cloned.1.call-done, f32[512]{0:T(512)S(1)} %add_rsqrt_fusion.1), kind=kOutput, calls=%fused_computation.24 | convolution fusion | flops 1357969408 | bytes 15476736 | tf_op jit(solution)/shard_map/pgjd,qgd->gjpq/dot_general | solution.py:22
  366.3 9.5 %fusion.6 = (f32[4,512]{1,0:T(4,128)S(1)}, f32[4,512]{1,0:T(4,128)S(1)}, f32[512,512,4]{1,0,2:T(8,128)}) fusion(f32[512,512,4]{1,0,2:T(8,128)} %get-tuple-element.14, f32[4,512]{1,0:T(4,128)S(1)} %get-tuple-element.13, pred[512,512]{0,1:T(8,128)(4,1)S(1)} %fusion.26, bf16[512,4,128]{0,2,1:T(8,128)(2,1)S(1)} %bitcast.121, bf16[4096,128]{1,0:T(8,128)(2,1)} %param.22, ...), kind=kOutput, calls=%fused_computation.26 | convolution fusion | flops 820047872 | bytes 14444544 | tf_op jit(solution)/shard_map/pgjd,qgd->gjpq/dot_general | solution.py:22
  375.7 3.2 fusion.7
  379.0 6.6 %fusion.17 = bf16[128,4,512]{2,0,1:T(8,128)(2,1)S(1)} fusion(f32[4,512]{1,0:T(4,128)S(1)} %fusion.7, f32[4,512]{1,0:T(4,128)S(1)} %get-tuple-element.8, f32[512,512,4]{1,0,2:T(8,128)} %get-tuple-element.15, pred[512,512]{0,1:T(8,128)(4,1)S(1)} %fusion.26, bf16[4096,128]{1,0:T(8,128)(2,1)} %param.23, bf16[512,4096]{1,0:T(8,128)(2,1)} %all-gather.16.cloned.1.call-done, ...), kind=kOutput, calls=%fused_computation.37 | convolution fusion | flops 818216960 | bytes 10242048 | tf_op jit(solution)/shard_map/gjpq,qgd->pgjd/dot_general | solution.py:31
  385.8 3.5 scatter_custom_fusion.1
  389.4 5.3 %all-to-all-start.4 = ((bf16[32,32,512]{2,1,0:T(8,128)(2,1)}), bf16[32,32,512]{2,1,0:T(8,128)(2,1)S(1)}, u32[]{:S(2)}, u32[]{:S(2)}) async-start(bf16[32,32,512]{2,1,0:T(8,128)(2,1)} %bitcast.113), calls=%async_computation.4 | async-start | bytes 2097152 | tf_op jit(solution)/shard_map/all_to_all | solution.py:110
  394.7 42.2 %all-gather.8.cloned.1.call-done = bf16[8192,128]{1,0:T(8,128)(2,1)} async-done(((bf16[256,128]{1,0:T(8,128)(2,1)}), bf16[8192,128]{1,0:T(8,128)(2,1)}) %all-gather.8.cloned.1.call-update) | async-done | bytes 2097168 | tf_op jit(solution)/shard_map/all_gather | solution.py:93
  436.9 9.9 %fusion.14 = bf16[128,4,512]{2,0,1:T(8,128)(2,1)} fusion(f32[4,512]{1,0:T(4,128)S(1)} %get-tuple-element.7, f32[4,512]{1,0:T(4,128)S(1)} %get-tuple-element.13, f32[512,512,4]{1,0,2:T(8,128)} %get-tuple-element.14, pred[512,512]{0,1:T(8,128)(4,1)S(1)} %fusion.26, bf16[8192,128]{1,0:T(8,128)(2,1)} %all-gather.8.cloned.1.call-done, ...), kind=kOutput, calls=%fused_computation.36 | convolution fusion | flops 1361379328 | bytes 15484928 | tf_op jit(solution)/shard_map/gjpq,qgd->pgjd/dot_general | solution.py:31
  446.8 2.1 copy.28
  448.9 4.0 scatter_custom_fusion
  452.9 6.5 %all-to-all-start.2 = ((bf16[32,32,512]{2,1,0:T(8,128)(2,1)}), bf16[32,32,512]{2,1,0:T(8,128)(2,1)}, u32[]{:S(2)}, u32[]{:S(2)}) async-start(bf16[32,32,512]{2,1,0:T(8,128)(2,1)} %bitcast.114), calls=%async_computation.2 | async-start | bytes 2097152 | tf_op jit(solution)/shard_map/all_to_all | solution.py:109
  459.5 1.8 gather_fusion.7
  461.3 19.5 %all-to-all-done.2 = bf16[32,32,512]{2,1,0:T(8,128)(2,1)} async-done(((bf16[32,32,512]{2,1,0:T(8,128)(2,1)}), bf16[32,32,512]{2,1,0:T(8,128)(2,1)}, u32[]{:S(2)}, u32[]{:S(2)}) %all-to-all-start.2) | async-done | bytes 1048608 | tf_op jit(solution)/shard_map/all_to_all | solution.py:109
  480.8 2.8 gather_fusion.5
  483.6 1.5 broadcast_select_fusion.3
  485.1 0.4 fusion.52
  485.5 0.4 fusion.53
  485.9 20.3 %psum.7 = f32[2,1024]{1,0:T(2,128)S(1)} all-reduce(f32[2,1024]{1,0:T(2,128)S(1)} %pad_maximum_fusion), channel_id=1, replica_groups=mesh['rep'=32,'tp'=8] {'tp'}, use_global_device_ids=true, to_apply=%region_10.12 | all-reduce | flops 2048 | bytes 16384 | tf_op jit(solution)/shard_map/psum | solution.py:124
  506.2 0.6 fusion.47
  (44 shorter events, 1.1 us)
Async XLA Ops:
  7.2 56.2 %copy-start = (bf16[1024,1024]{1,0:T(8,128)(2,1)S(1)}, bf16[1024,1024]{1,0:T(8,128)(2,1)}, u32[]{:S(2)}) copy-start(bf16[1024,1024]{1,0:T(8,128)(2,1)} %param.14) | copy-start | bytes 6291460
  11.6 20.7 %all-to-all-start = ((s32[32,32,1]{1,2,0:T(1,128)}), s32[32,32,1]{1,2,0:T(1,128)S(1)}, u32[]{:S(2)}, u32[]{:S(2)}) async-start(s32[32,32,1]{1,2,0:T(1,128)} %bitcast.2), calls=%async_computation | async-start | bytes 32768 | tf_op jit(solution)/shard_map/all_to_all | solution.py:74
  32.3 28.3 %all-to-all-start.3 = ((bf16[32,32,512]{2,1,0:T(8,128)(2,1)}), bf16[32,32,512]{2,1,0:T(8,128)(2,1)S(1)}, u32[]{:S(2)}, u32[]{:S(2)}) async-start(bf16[32,32,512]{2,1,0:T(8,128)(2,1)} %broadcast_select_fusion.1), calls=%async_computation.3 | async-start | bytes 2097152 | tf_op jit(solution)/shard_map/all_to_all | solution.py:73
  36.2 96.4 %all-gather.16.cloned.1.call-start = ((), (), s32[]{:S(2)}) async-start(), calls=%async_computation.9 | async-start | bytes 4718592 | tf_op jit(solution)/shard_map/all_gather | solution.py:80
  63.3 118.3 %all-gather.14.cloned.1.call-start = ((), (), s32[]{:S(2)}) async-start(), calls=%async_computation.8 | async-start | bytes 9437184 | tf_op jit(solution)/shard_map/all_gather | solution.py:79
  127.7 154.4 %all-gather.12.cloned.1.call-start = ((), (), s32[]{:S(2)}) async-start(), calls=%async_computation.7 | async-start | bytes 8650752 | tf_op jit(solution)/shard_map/all_gather | solution.py:91
  128.4 227.6 %all-gather.10.cloned.1.call-start = ((), (), s32[]{:S(2)}) async-start(), calls=%async_computation.6 | async-start | bytes 2162688 | tf_op jit(solution)/shard_map/all_gather | solution.py:92
  129.0 307.9 %all-gather.8.cloned.1.call-start = ((), (), s32[]{:S(2)}) async-start(), calls=%async_computation.5 | async-start | bytes 2162688 | tf_op jit(solution)/shard_map/all_gather | solution.py:93
  132.6 3.5 copy-start.2
  389.4 63.5 %all-to-all-start.4 = ((bf16[32,32,512]{2,1,0:T(8,128)(2,1)}), bf16[32,32,512]{2,1,0:T(8,128)(2,1)S(1)}, u32[]{:S(2)}, u32[]{:S(2)}) async-start(bf16[32,32,512]{2,1,0:T(8,128)(2,1)} %bitcast.113), calls=%async_computation.4 | async-start | bytes 2097152 | tf_op jit(solution)/shard_map/all_to_all | solution.py:110
  446.8 12.6 %copy-start.4 = (bf16[512]{0:T(512)(128)(2,1)S(1)}, bf16[512]{0:T(512)(128)(2,1)}, u32[]{:S(2)}) copy-start(bf16[512]{0:T(512)(128)(2,1)} %param.24) | copy-start | bytes 3076
  446.8 12.6 %copy-start.5 = (bf16[512]{0:T(512)(128)(2,1)S(1)}, bf16[512]{0:T(512)(128)(2,1)}, u32[]{:S(2)}) copy-start(bf16[512]{0:T(512)(128)(2,1)} %param.25) | copy-start | bytes 3076
  446.8 12.6 %copy-start.6 = (s32[1,32]{1,0:T(1,128)S(1)}, s32[1,32]{1,0:T(1,128)}, u32[]{:S(2)}) copy-start(s32[1,32]{1,0:T(1,128)} %param.17) | copy-start | bytes 388
  446.8 12.7 %copy-start.3 = (s32[1024]{0:T(1024)S(1)}, s32[1024]{0:T(1024)}, u32[]{:S(2)}) copy-start(s32[1024]{0:T(1024)} %param.16) | copy-start | bytes 12292
  452.9 6.6 %copy-start.1 = (bf16[32,32,512]{2,1,0:T(8,128)(2,1)}, bf16[32,32,512]{2,1,0:T(8,128)(2,1)S(1)}, u32[]{:S(2)}) copy-start(bf16[32,32,512]{2,1,0:T(8,128)(2,1)S(1)} %all-to-all-done.4) | copy-start | bytes 3145732
  452.9 27.9 %all-to-all-start.2 = ((bf16[32,32,512]{2,1,0:T(8,128)(2,1)}), bf16[32,32,512]{2,1,0:T(8,128)(2,1)}, u32[]{:S(2)}, u32[]{:S(2)}) async-start(bf16[32,32,512]{2,1,0:T(8,128)(2,1)} %bitcast.114), calls=%async_computation.2 | async-start | bytes 2097152 | tf_op jit(solution)/shard_map/all_to_all | solution.py:109
Sparse Core Ops, SparseCore 0:
  63.4 36.1 all-gather.15
  127.8 53.6 all-gather.13
  184.1 97.8 all-gather.11
  284.5 71.5 all-gather.9
  358.5 78.3 all-gather.7
where the time goes:
time: 519 us; the launch traced here: 514 us
  waiting for transfers between devices  287 us (55%)
  blocking collectives  75.4 us (15%)
  matrix products  52.9 us (10%)
  local copies, waits for them, and re-layouts  31.9 us (6%)
  starting transfers between devices  27.9 us (5%)
  other arithmetic  24.5 us (5%)
  between operations  14.3 us (3%)
    all_gather x1, waiting for transfers between devices, body(): lax.all_gather(ref_query, 'rep', axis=0, tiled=True)  95.4 us
    all_gather x1, waiting for transfers between devices, body(): lax.all_gather(ref_key, 'rep', axis=0, tiled=True)  62.8 us
    all_to_all x1, blocking collectives, body(): lax.all_to_all(by_pack(reference_rows), 'rep', split_axis=0, concat_axis=...  55.1 us
    all_gather x1, waiting for transfers between devices, body(): lax.all_gather(ref_value, 'rep', axis=0, tiled=True)  42.2 us
    all_gather x1, waiting for transfers between devices, body(): lax.all_gather(ref_in[chosen], 'tp', axis=1, tiled=True)  40.8 us
    psum x1, blocking collectives, body(): ordered = lax.psum(partial_value, 'tp')  20.3 us
    dot_general x2, matrix products, attend(): jnp.einsum('pgjd,qgd->gjpq', query_four, key_three, preferred_element_typ...  19.7 us
    all_to_all x1, waiting for transfers between devices, body(): lax.all_to_all(ref_spread, 'rep', split_axis=0, concat_axis=0, tiled=True)  19.5 us
  transfers between devices with their start and end apart: 9, of which 7 were waited for; matrix products, arithmetic and copies ran while one was open for 19% of the time, Pallas kernels for 0%

commit v1 on v0

--- a/solution.py
+++ b/solution.py
@@ -121,7 +121,7 @@
             jnp.dot(critic_home, critic_readout, preferred_element_type=jnp.float32),
         ]
     )
-    ordered = lax.psum(partial_value, "tp")
+    ordered = jnp.sum(lax.all_gather(partial_value, "tp"), axis=0)
     ordered = jnp.where(segment_ids[None, :] >= 0, ordered, 0.0)
     return (ordered[0], ordered[1])
 

time: 519 us -> 520 us (level)
    all_gather x0 -> x1, blocking collectives: none -> 21 us  [body(): ordered = jnp.sum(lax.all_gather(partial_value, 'tp'), axis=0)]
    psum x1 -> x0, blocking collectives: 20.3 us -> none  [body(): ordered = lax.psum(partial_value, 'tp')]
where the time goes in v1:
time: 520 us; the launch traced here: 514 us
  waiting for transfers between devices  287 us (55%)
  blocking collectives  76.1 us (15%)
  matrix products  52.9 us (10%)
  local copies, waits for them, and re-layouts  31.9 us (6%)
  starting transfers between devices  27.9 us (5%)
  other arithmetic  24.5 us (5%)
  between operations  14.3 us (3%)
    all_gather x1, waiting for transfers between devices, body(): lax.all_gather(ref_query, 'rep', axis=0, tiled=True)  95.4 us
    all_gather x1, waiting for transfers between devices, body(): lax.all_gather(ref_key, 'rep', axis=0, tiled=True)  62.8 us
    all_to_all x1, blocking collectives, body(): lax.all_to_all(by_pack(reference_rows), 'rep', split_axis=0, concat_axis=...  55.1 us
    all_gather x1, waiting for transfers between devices, body(): lax.all_gather(ref_value, 'rep', axis=0, tiled=True)  42.2 us
    all_gather x1, waiting for transfers between devices, body(): lax.all_gather(ref_in[chosen], 'tp', axis=1, tiled=True)  40.8 us
    all_gather x1, blocking collectives, body(): ordered = jnp.sum(lax.all_gather(partial_value, 'tp'), axis=0)  21 us
    dot_general x2, matrix products, attend(): jnp.einsum('pgjd,qgd->gjpq', query_four, key_three, preferred_element_typ...  19.7 us
    all_to_all x1, waiting for transfers between devices, body(): lax.all_to_all(ref_spread, 'rep', split_axis=0, concat_axis=0, tiled=True)  19.5 us
  transfers between devices with their start and end apart: 9, of which 7 were waited for; matrix products, arithmetic and copies ran while one was open for 19% of the time, Pallas kernels for 0%

profile of v1, /device:TPU:1, one launch (start us, length us, event | category | flops | bytes accessed | tf_op | source)
XLA Modules:
  0.0 514.3 jit_solution(6853609630676666132)
XLA Ops:
  7.2 2.4 sort.34
  9.6 0.8 reshape.165
  10.4 0.6 gather_fusion
  10.9 0.7 bitcast_select_fusion.2
  11.6 12.0 %all-to-all-start = ((s32[32,32,1]{1,2,0:T(1,128)}), s32[32,32,1]{1,2,0:T(1,128)S(1)}, u32[]{:S(2)}, u32[]{:S(2)}) async-start(s32[32,32,1]{1,2,0:T(1,128)} %bitcast.2), calls=%async_computation | async-start | bytes 32768 | tf_op jit(solution)/shard_map/all_to_all | solution.py:74
  23.7 1.8 gather_fusion.6
  25.5 1.2 broadcast_select_fusion.1
  26.7 5.6 %all-to-all-done = s32[32,32,1]{1,2,0:T(1,128)S(1)} async-done(((s32[32,32,1]{1,2,0:T(1,128)}), s32[32,32,1]{1,2,0:T(1,128)S(1)}, u32[]{:S(2)}, u32[]{:S(2)}) %all-to-all-start) | async-done | bytes 4128 | tf_op jit(solution)/shard_map/all_to_all | solution.py:74
  32.3 3.9 all-to-all-start.3
  36.3 0.5 broadcast.155
  36.8 0.7 reduce.8
  37.6 4.4 sort.35
  41.9 18.7 %all-to-all-done.3 = bf16[32,32,512]{2,1,0:T(8,128)(2,1)S(1)} async-done(((bf16[32,32,512]{2,1,0:T(8,128)(2,1)}), bf16[32,32,512]{2,1,0:T(8,128)(2,1)S(1)}, u32[]{:S(2)}, u32[]{:S(2)}) %all-to-all-start.3) | async-done | bytes 1048608 | tf_op jit(solution)/shard_map/all_to_all | solution.py:73
  60.6 2.6 gather_fusion.4
  63.3 2.0 gather_fusion.1
  65.4 1.8 broadcast_select_fusion
  67.2 55.1 %all_to_all.45 = bf16[32,32,1024]{2,1,0:T(8,128)(2,1)} all-to-all(bf16[32,32,1024]{2,1,0:T(8,128)(2,1)S(1)} %broadcast_select_fusion), channel_id=1, replica_groups=mesh['rep'=32,'tp'=8] {'rep'}, dimensions={0} | all-to-all | bytes 4194304 | tf_op jit(solution)/shard_map/all_to_all | solution.py:72
  122.3 5.4 %gather_fusion.2 = bf16[512,1024]{1,0:T(8,128)(2,1)} fusion(bf16[1024,1024]{1,0:T(8,128)(2,1)} %bitcast.111, s32[1024]{0:T(1024)S(1)} %pad_clamp_fusion.1), kind=kCustom, calls=%fused_computation.5 | custom fusion | bytes 2099200 | tf_op jit(solution)/shard_map/gather | solution.py:79
  127.7 0.7 all-gather.14.cloned.1.call-update
  128.5 0.5 all-gather.12.cloned.1.call-update
  129.0 0.5 all-gather.10.cloned.1.call-update
  129.6 2.8 gather_fusion.3
  132.6 3.2 fusion.2
  136.0 4.7 convolution_convert_fusion
  140.8 40.8 %all-gather.16.cloned.1.call-done = bf16[512,8192]{1,0:T(8,128)(2,1)} async-done(((bf16[512,1024]{1,0:T(8,128)(2,1)}), bf16[512,8192]{1,0:T(8,128)(2,1)}) %all-gather.16.cloned.1.call-update) | async-done | bytes 8388624 | tf_op jit(solution)/shard_map/all_gather | solution.py:79
  181.5 5.1 fusion
  186.6 95.4 %all-gather.14.cloned.1.call-done = bf16[8192,512]{1,0:T(8,128)(2,1)} async-done(((bf16[256,512]{1,0:T(8,128)(2,1)}), bf16[8192,512]{1,0:T(8,128)(2,1)}) %all-gather.14.cloned.1.call-update) | async-done | bytes 8388624 | tf_op jit(solution)/shard_map/all_gather | solution.py:91
  282.1 11.2 %convolution_convert_fusion.1 = bf16[512,512]{0,1:T(8,128)(2,1)} fusion(bf16[8192,512]{1,0:T(8,128)(2,1)} %all-gather.14.cloned.1.call-done, bf16[512,8192]{1,0:T(8,128)(2,1)} %all-gather.16.cloned.1.call-done, f32[512]{0:T(512)S(1)} %add_rsqrt_fusion.1), kind=kOutput, calls=%fused_computation.38 | convolution fusion | flops 4307812352 | bytes 17303552 | tf_op jit(solution)/shard_map/dot_general | solution.py:97
  293.3 62.8 %all-gather.12.cloned.1.call-done = bf16[8192,128]{1,0:T(8,128)(2,1)} async-done(((bf16[256,128]{1,0:T(8,128)(2,1)}), bf16[8192,128]{1,0:T(8,128)(2,1)}) %all-gather.12.cloned.1.call-update) | async-done | bytes 2097168 | tf_op jit(solution)/shard_map/all_gather | solution.py:92
  356.1 10.2 %fusion.4 = (f32[4,512]{1,0:T(4,128)S(1)}, f32[512,512,4]{1,0,2:T(8,128)}) fusion(pred[512,512]{0,1:T(8,128)(4,1)S(1)} %fusion.26, bf16[512,4,128]{0,2,1:T(8,128)(2,1)} %bitcast.124, bf16[8192,128]{1,0:T(8,128)(2,1)} %all-gather.12.cloned.1.call-done, bf16[512,8192]{1,0:T(8,128)(2,1)} %all-gather.16.cloned.1.call-done, f32[512]{0:T(512)S(1)} %add_rsqrt_fusion.1), kind=kOutput, calls=%fused_computation.24 | convolution fusion | flops 1357969408 | bytes 15476736 | tf_op jit(solution)/shard_map/pgjd,qgd->gjpq/dot_general | solution.py:22
  366.3 9.5 %fusion.6 = (f32[4,512]{1,0:T(4,128)S(1)}, f32[4,512]{1,0:T(4,128)S(1)}, f32[512,512,4]{1,0,2:T(8,128)}) fusion(f32[512,512,4]{1,0,2:T(8,128)} %get-tuple-element.14, f32[4,512]{1,0:T(4,128)S(1)} %get-tuple-element.13, pred[512,512]{0,1:T(8,128)(4,1)S(1)} %fusion.26, bf16[512,4,128]{0,2,1:T(8,128)(2,1)S(1)} %bitcast.123, bf16[4096,128]{1,0:T(8,128)(2,1)} %param.22, ...), kind=kOutput, calls=%fused_computation.26 | convolution fusion | flops 820047872 | bytes 14444544 | tf_op jit(solution)/shard_map/pgjd,qgd->gjpq/dot_general | solution.py:22
  375.7 3.2 fusion.7
  379.0 6.6 %fusion.17 = bf16[128,4,512]{2,0,1:T(8,128)(2,1)S(1)} fusion(f32[4,512]{1,0:T(4,128)S(1)} %fusion.7, f32[4,512]{1,0:T(4,128)S(1)} %get-tuple-element.8, f32[512,512,4]{1,0,2:T(8,128)} %get-tuple-element.15, pred[512,512]{0,1:T(8,128)(4,1)S(1)} %fusion.26, bf16[4096,128]{1,0:T(8,128)(2,1)} %param.23, bf16[512,4096]{1,0:T(8,128)(2,1)} %all-gather.18.cloned.1.call-done, ...), kind=kOutput, calls=%fused_computation.37 | convolution fusion | flops 818216960 | bytes 10242048 | tf_op jit(solution)/shard_map/gjpq,qgd->pgjd/dot_general | solution.py:31
  385.8 3.5 scatter_custom_fusion.1
  389.4 5.3 %all-to-all-start.4 = ((bf16[32,32,512]{2,1,0:T(8,128)(2,1)}), bf16[32,32,512]{2,1,0:T(8,128)(2,1)S(1)}, u32[]{:S(2)}, u32[]{:S(2)}) async-start(bf16[32,32,512]{2,1,0:T(8,128)(2,1)} %bitcast.115), calls=%async_computation.4 | async-start | bytes 2097152 | tf_op jit(solution)/shard_map/all_to_all | solution.py:110
  394.7 42.2 %all-gather.10.cloned.1.call-done = bf16[8192,128]{1,0:T(8,128)(2,1)} async-done(((bf16[256,128]{1,0:T(8,128)(2,1)}), bf16[8192,128]{1,0:T(8,128)(2,1)}) %all-gather.10.cloned.1.call-update) | async-done | bytes 2097168 | tf_op jit(solution)/shard_map/all_gather | solution.py:93
  436.9 9.9 %fusion.14 = bf16[128,4,512]{2,0,1:T(8,128)(2,1)} fusion(f32[4,512]{1,0:T(4,128)S(1)} %get-tuple-element.7, f32[4,512]{1,0:T(4,128)S(1)} %get-tuple-element.13, f32[512,512,4]{1,0,2:T(8,128)} %get-tuple-element.14, pred[512,512]{0,1:T(8,128)(4,1)S(1)} %fusion.26, bf16[8192,128]{1,0:T(8,128)(2,1)} %all-gather.10.cloned.1.call-done, ...), kind=kOutput, calls=%fused_computation.36 | convolution fusion | flops 1361379328 | bytes 15484928 | tf_op jit(solution)/shard_map/gjpq,qgd->pgjd/dot_general | solution.py:31
  446.8 2.1 copy.28
  448.9 4.0 scatter_custom_fusion
  452.9 6.5 %all-to-all-start.2 = ((bf16[32,32,512]{2,1,0:T(8,128)(2,1)}), bf16[32,32,512]{2,1,0:T(8,128)(2,1)}, u32[]{:S(2)}, u32[]{:S(2)}) async-start(bf16[32,32,512]{2,1,0:T(8,128)(2,1)} %bitcast.116), calls=%async_computation.2 | async-start | bytes 2097152 | tf_op jit(solution)/shard_map/all_to_all | solution.py:109
  459.5 1.8 gather_fusion.7
  461.3 19.5 %all-to-all-done.2 = bf16[32,32,512]{2,1,0:T(8,128)(2,1)} async-done(((bf16[32,32,512]{2,1,0:T(8,128)(2,1)}), bf16[32,32,512]{2,1,0:T(8,128)(2,1)}, u32[]{:S(2)}, u32[]{:S(2)}) %all-to-all-start.2) | async-done | bytes 1048608 | tf_op jit(solution)/shard_map/all_to_all | solution.py:109
  480.8 2.8 gather_fusion.5
  483.6 1.5 broadcast_select_fusion.3
  485.1 0.4 fusion.52
  485.5 0.4 fusion.53
  485.9 21.0 %all-gather.3 = f32[8,2,1024]{2,1,0:T(2,128)S(1)} all-gather(f32[1,2,1024]{2,1,0:T(2,128)S(1)} %maximum_bitcast_fusion), channel_id=4, replica_groups=mesh['rep'=32,'tp'=8] {'tp'}, dimensions={0}, use_global_device_ids=true | all-gather | bytes 73728 | tf_op jit(solution)/shard_map/all_gather | solution.py:124
  507.0 0.6 fusion.47
  (45 shorter events, 1.1 us)
Async XLA Ops:
  7.2 56.2 %copy-start = (bf16[1024,1024]{1,0:T(8,128)(2,1)S(1)}, bf16[1024,1024]{1,0:T(8,128)(2,1)}, u32[]{:S(2)}) copy-start(bf16[1024,1024]{1,0:T(8,128)(2,1)} %param.14) | copy-start | bytes 6291460
  11.6 20.7 %all-to-all-start = ((s32[32,32,1]{1,2,0:T(1,128)}), s32[32,32,1]{1,2,0:T(1,128)S(1)}, u32[]{:S(2)}, u32[]{:S(2)}) async-start(s32[32,32,1]{1,2,0:T(1,128)} %bitcast.2), calls=%async_computation | async-start | bytes 32768 | tf_op jit(solution)/shard_map/all_to_all | solution.py:74
  32.3 28.3 %all-to-all-start.3 = ((bf16[32,32,512]{2,1,0:T(8,128)(2,1)}), bf16[32,32,512]{2,1,0:T(8,128)(2,1)S(1)}, u32[]{:S(2)}, u32[]{:S(2)}) async-start(bf16[32,32,512]{2,1,0:T(8,128)(2,1)} %broadcast_select_fusion.1), calls=%async_computation.3 | async-start | bytes 2097152 | tf_op jit(solution)/shard_map/all_to_all | solution.py:73
  36.2 96.4 %all-gather.18.cloned.1.call-start = ((), (), s32[]{:S(2)}) async-start(), calls=%async_computation.9 | async-start | bytes 4718592 | tf_op jit(solution)/shard_map/all_gather | solution.py:80
  63.3 118.3 %all-gather.16.cloned.1.call-start = ((), (), s32[]{:S(2)}) async-start(), calls=%async_computation.8 | async-start | bytes 9437184 | tf_op jit(solution)/shard_map/all_gather | solution.py:79
  127.7 154.4 %all-gather.14.cloned.1.call-start = ((), (), s32[]{:S(2)}) async-start(), calls=%async_computation.7 | async-start | bytes 8650752 | tf_op jit(solution)/shard_map/all_gather | solution.py:91
  128.4 227.6 %all-gather.12.cloned.1.call-start = ((), (), s32[]{:S(2)}) async-start(), calls=%async_computation.6 | async-start | bytes 2162688 | tf_op jit(solution)/shard_map/all_gather | solution.py:92
  129.0 307.9 %all-gather.10.cloned.1.call-start = ((), (), s32[]{:S(2)}) async-start(), calls=%async_computation.5 | async-start | bytes 2162688 | tf_op jit(solution)/shard_map/all_gather | solution.py:93
  132.6 3.5 copy-start.2
  389.4 63.5 %all-to-all-start.4 = ((bf16[32,32,512]{2,1,0:T(8,128)(2,1)}), bf16[32,32,512]{2,1,0:T(8,128)(2,1)S(1)}, u32[]{:S(2)}, u32[]{:S(2)}) async-start(bf16[32,32,512]{2,1,0:T(8,128)(2,1)} %bitcast.115), calls=%async_computation.4 | async-start | bytes 2097152 | tf_op jit(solution)/shard_map/all_to_all | solution.py:110
  446.8 12.6 %copy-start.4 = (bf16[512]{0:T(512)(128)(2,1)S(1)}, bf16[512]{0:T(512)(128)(2,1)}, u32[]{:S(2)}) copy-start(bf16[512]{0:T(512)(128)(2,1)} %param.24) | copy-start | bytes 3076
  446.8 12.6 %copy-start.5 = (bf16[512]{0:T(512)(128)(2,1)S(1)}, bf16[512]{0:T(512)(128)(2,1)}, u32[]{:S(2)}) copy-start(bf16[512]{0:T(512)(128)(2,1)} %param.25) | copy-start | bytes 3076
  446.8 12.6 %copy-start.6 = (s32[1,32]{1,0:T(1,128)S(1)}, s32[1,32]{1,0:T(1,128)}, u32[]{:S(2)}) copy-start(s32[1,32]{1,0:T(1,128)} %param.17) | copy-start | bytes 388
  446.8 12.7 %copy-start.3 = (s32[1024]{0:T(1024)S(1)}, s32[1024]{0:T(1024)}, u32[]{:S(2)}) copy-start(s32[1024]{0:T(1024)} %param.16) | copy-start | bytes 12292
  452.9 6.6 %copy-start.1 = (bf16[32,32,512]{2,1,0:T(8,128)(2,1)}, bf16[32,32,512]{2,1,0:T(8,128)(2,1)S(1)}, u32[]{:S(2)}) copy-start(bf16[32,32,512]{2,1,0:T(8,128)(2,1)S(1)} %all-to-all-done.4) | copy-start | bytes 3145732
  452.9 27.9 %all-to-all-start.2 = ((bf16[32,32,512]{2,1,0:T(8,128)(2,1)}), bf16[32,32,512]{2,1,0:T(8,128)(2,1)}, u32[]{:S(2)}, u32[]{:S(2)}) async-start(bf16[32,32,512]{2,1,0:T(8,128)(2,1)} %bitcast.116), calls=%async_computation.2 | async-start | bytes 2097152 | tf_op jit(solution)/shard_map/all_to_all | solution.py:109
Sparse Core Ops, SparseCore 0:
  63.4 36.1 all-gather.17
  127.8 53.6 all-gather.15
  184.1 97.8 all-gather.13
  284.5 71.5 all-gather.11
  358.5 78.3 all-gather.9
